TPU v7x, 512 devices: a whole 4x4x16 slice. The times are simulated.
512 devices in a mesh: docs: 64 (over x, z_lo, core), blk: 8 (over y, z_hi).
Axes of the slice: x: 4, y: 4, z: 16 (z_hi: 2, z_lo: 8; z = z_hi * 8 + z_lo), core: 2. Of those that a mesh axis runs over, the one named last changes fastest.
Arguments:
- group_rows: bfloat16 [8, 16384, 2048], P('blk', 'docs'), may hold values from -0.14941406 to 0.14941406
- group_owner: int32 [8, 16384, 1], P('blk', 'docs'), may hold values from 0 to 63; in each aligned block of 256 rows (0 to 255, 256 to 511, ..., all dimensions but the last counted through in order) at most 8 rows name the same one
- group_doc: int32 [8, 16384], P('blk', 'docs'), may hold values from 0 to 255
- doc_weight: float32 [8, 16384], P('blk', 'docs'), may hold values from 0.1 to 1
- queries: bfloat16 [256, 2048], P('blk'), may hold values from -6 to 6
- precond: bfloat16 [2048, 2048], P(None, 'docs'), may hold values from -0.125 to 0.125
Outputs:
- scores: float32 [256, 8, 16384], P(None, 'blk', 'docs')
Inputs may be any that keep to these rules, and one draw needn't show every extreme that they name: `group_owner`: within the rows of one device, at most 8 groups name the same owner, and some owner gets exactly 8.
All inputs are finite; a program needn't handle non-finite values.
Results may differ from a plain program's by a relative error of at most 0.006.
Values may be sent and summed in bfloat16 or wider, within the bound.
A program may use at most 64 MiB of HBM per device.

v0:
```python
import jax
import jax.numpy as jnp
from jax import lax
from jax.sharding import PartitionSpec as P


def against_docs(left, high_part, low_part, weight):
    dims = (((1,), (1,)), ((), ()))
    product = lax.dot_general(left, high_part, dims, preferred_element_type=jnp.float32)
    product = product + lax.dot_general(left, low_part, dims, preferred_element_type=jnp.float32)
    return product * weight[None, :]


def shards(group_rows, group_owner, group_doc, doc_weight, queries, precond):
    rows = group_rows[0]
    owner = group_owner[0, :, 0]
    doc_index = group_doc[0]
    peers = lax.axis_size("docs")
    count = rows.shape[0]
    width = rows.shape[1]
    capacity = 2 * count // peers
    peer_ids = jnp.arange(peers, dtype=jnp.int32)
    owner_table = (owner[:, None] == peer_ids[None, :]).astype(jnp.int32)
    earlier = jnp.cumsum(owner_table, axis=0) - owner_table
    slot = jnp.sum(earlier * owner_table, axis=1)
    send_ids = jnp.full((peers, capacity), -1, jnp.int32).at[owner, slot].set(doc_index)
    doc_count = doc_weight.shape[1]
    doc_ids = jnp.arange(doc_count, dtype=jnp.int32)
    weight = doc_weight[0]
    query_pre = jnp.dot(queries, precond, preferred_element_type=jnp.float32).astype(jnp.bfloat16)
    send_rows = jnp.zeros((peers, capacity, width), jnp.bfloat16).at[owner, slot].set(rows)
    got_rows, got_ids = (
        lax.all_to_all(send_rows, "docs", split_axis=0, concat_axis=0, tiled=True),
        lax.all_to_all(send_ids, "docs", split_axis=0, concat_axis=0, tiled=True),
    )
    got_rows = got_rows.reshape(peers * capacity, width)
    got_ids = got_ids.reshape(peers * capacity)
    member_table = (doc_ids[:, None] == got_ids[None, :]).astype(jnp.bfloat16)
    doc_print = jnp.dot(member_table, got_rows, preferred_element_type=jnp.float32)
    high_part = doc_print.astype(jnp.bfloat16)
    low_part = (doc_print - high_part.astype(jnp.float32)).astype(jnp.bfloat16)
    full_rows = lax.all_gather(query_pre, "docs", axis=1, tiled=True)
    scores = against_docs(
        lax.all_gather(full_rows, "blk", axis=0, tiled=True), high_part, low_part, weight
    )
    return scores[:, None, :]


def solution(mesh):
    return jax.shard_map(
        shards,
        mesh=mesh,
        in_specs=(
            P("blk", "docs", None),
            P("blk", "docs", None),
            P("blk", "docs"),
            P("blk", "docs"),
            P("blk", None),
            P(None, "docs"),
        ),
        out_specs=P(None, "blk", "docs"),
        check_vma=False,
    )
```

profile of v0, /device:TPU:2, one launch (start us, length us, event | category | flops | bytes accessed | tf_op | source)
XLA Modules:
  0.0 392.6 jit_solution(211520665865208457)
XLA Ops:
  6.5 0.0 copy-start
  6.5 0.7 fusion.11
  7.3 0.6 reduce-window.6
  7.9 0.2 slice_reduce_fusion
  8.1 0.8 fusion.10
  8.9 0.7 or_select_fusion
  9.6 0.0 copy-start.2
  9.6 21.2 %scatter_fusion = s32[64,8]{0,1:T(8,128)S(1)} fusion(s32[64,8]{0,1:T(8,128)S(1)} %broadcast_in_dim.6, s32[256]{0:T(256)S(1)} %bitcast.39, s32[256]{0:T(256)} %bitcast.45), kind=kCustom, calls=%fused_computation | custom fusion | bytes 5120 | tf_op jit(solution)/shard_map/scatter | solution.py:26
  30.8 0.7 copy.18
  31.5 16.1 %all-to-all-start = ((s32[64,1,8]{2,1,0:T(1,128)}), s32[64,1,8]{2,1,0:T(1,128)S(1)}, u32[]{:S(2)}, u32[]{:S(2)}) async-start(s32[64,1,8]{2,1,0:T(1,128)} %copy.18), calls=%async_computation | async-start | bytes 65536 | tf_op jit(solution)/shard_map/all_to_all | solution.py:34
  47.6 1.6 broadcast_in_dim.7
  49.2 0.0 copy-done.2
  49.2 44.4 %scatter_fusion.1 = bf16[64,8,2048]{2,1,0:T(8,128)(2,1)} fusion(bf16[64,8,2048]{2,1,0:T(8,128)(2,1)} %broadcast_in_dim.7, s32[256]{0:T(256)S(1)} %bitcast.40, bf16[256,2048]{1,0:T(8,128)(2,1)S(1)} %bitcast.41), kind=kCustom, calls=%fused_computation.1 | custom fusion | bytes 3147776 | tf_op jit(solution)/shard_map/scatter | solution.py:31
  93.6 0.0 all-to-all-done
  93.6 13.4 %all-to-all-start.1 = ((bf16[64,8,2048]{2,1,0:T(8,128)(2,1)}), bf16[64,8,2048]{2,1,0:T(8,128)(2,1)}, u32[]{:S(2)}, u32[]{:S(2)}) async-start(bf16[64,8,2048]{2,1,0:T(8,128)(2,1)} %scatter_fusion.1), calls=%async_computation.1 | async-start | bytes 4194304 | tf_op jit(solution)/shard_map/all_to_all | solution.py:33
  107.0 0.0 all-gather.2.cloned.1.call-start
  107.0 0.0 copy-done
  107.0 0.2 convolution_convert_fusion
  107.2 0.1 copy.15
  107.3 181.2 %all_gather.6 = bf16[32,2048]{0,1:T(8,128)(2,1)S(1)} all-gather(bf16[32,32]{0,1:T(8,128)(2,1)S(1)} %copy.15), channel_id=1, replica_groups=mesh['docs'=64,'blk'=8] {'docs'}, dimensions={1}, use_global_device_ids=true | all-gather | bytes 133120 | tf_op jit(solution)/shard_map/all_gather | solution.py:42
  288.5 0.8 copy.16
  289.4 0.0 all-gather.2.cloned.1.call-update
  289.4 0.5 broadcast.101
  289.9 0.7 reduce.5
  290.6 0.1 eq.49
  290.7 0.0 all-to-all-done.1
  290.7 2.3 fusion
  293.1 0.0 copy-start.4
  293.1 89.4 %all-gather.2.cloned.1.call-done = bf16[256,2048]{1,0:T(8,128)(2,1)} async-done(((bf16[32,2048]{1,0:T(8,128)(2,1)}), bf16[256,2048]{1,0:T(8,128)(2,1)}) %all-gather.2.cloned.1.call-update) | async-done | bytes 1048592 | tf_op jit(solution)/shard_map/all_gather | solution.py:44
  382.5 1.8 fusion.5
  384.3 0.5 fusion.3
  384.8 1.0 copy.19
  (8 shorter events, 0.1 us)
Async XLA Ops:
  6.5 100.5 %copy-start = (bf16[32,2048]{1,0:T(8,128)(2,1)S(1)}, bf16[32,2048]{1,0:T(8,128)(2,1)}, u32[]{:S(2)}) copy-start(bf16[32,2048]{1,0:T(8,128)(2,1)} %param.10) | copy-start | bytes 393220
  9.6 39.6 %copy-start.2 = (bf16[1,256,2048]{2,1,0:T(8,128)(2,1)S(1)}, bf16[1,256,2048]{2,1,0:T(8,128)(2,1)}, u32[]{:S(2)}) copy-start(bf16[1,256,2048]{2,1,0:T(8,128)(2,1)} %param.6) | copy-start | bytes 3145732
  31.5 62.1 %all-to-all-start = ((s32[64,1,8]{2,1,0:T(1,128)}), s32[64,1,8]{2,1,0:T(1,128)S(1)}, u32[]{:S(2)}, u32[]{:S(2)}) async-start(s32[64,1,8]{2,1,0:T(1,128)} %copy.18), calls=%async_computation | async-start | bytes 65536 | tf_op jit(solution)/shard_map/all_to_all | solution.py:34
  93.6 13.4 %copy-start.3 = (bf16[2048,32]{0,1:T(8,128)(2,1)S(1)}, bf16[2048,32]{0,1:T(8,128)(2,1)}, u32[]{:S(2)}) copy-start(bf16[2048,32]{0,1:T(8,128)(2,1)} %param.11) | copy-start | bytes 393220
  93.6 197.1 %all-to-all-start.1 = ((bf16[64,8,2048]{2,1,0:T(8,128)(2,1)}), bf16[64,8,2048]{2,1,0:T(8,128)(2,1)}, u32[]{:S(2)}, u32[]{:S(2)}) async-start(bf16[64,8,2048]{2,1,0:T(8,128)(2,1)} %scatter_fusion.1), calls=%async_computation.1 | async-start | bytes 4194304 | tf_op jit(solution)/shard_map/all_to_all | solution.py:33
  107.0 275.5 %all-gather.2.cloned.1.call-start = ((), (), s32[]{:S(2)}) async-start(), calls=%async_computation.2 | async-start | bytes 1179648 | tf_op jit(solution)/shard_map/all_gather | solution.py:44
  293.1 91.2 %copy-start.4 = (f32[1,256]{1,0:T(1,128)S(1)}, f32[1,256]{1,0:T(1,128)}, u32[]{:S(2)}) copy-start(f32[1,256]{1,0:T(1,128)} %param.9) | copy-start | bytes 3076
  382.5 1.8 copy-start.1
Sparse Core Ops, SparseCore 0:
  289.5 92.9 all-gather.1
where the time goes:
time: 395 us; the launch traced here: 393 us
  blocking collectives  181 us (46%)
  waiting for transfers between devices  89.4 us (23%)
  local copies, waits for them, and re-layouts  70.6 us (18%)
  starting transfers between devices  29.5 us (7%)
  between operations  13.5 us (3%)
  matrix products  4.72 us (1%)
    all_gather x1, blocking collectives, shards(): full_rows = lax.all_gather(query_pre, 'docs', axis=1, tiled=True)  181 us
    all_gather x1, waiting for transfers between devices, shards(): lax.all_gather(full_rows, 'blk', axis=0, tiled=True)  89.4 us
    scatter x1, local copies, waits for them, and re-layouts, shards(): jnp.zeros((peers, capacity, width), jnp.bfloat16).at[owner, slot].set(rows)  44.4 us
    scatter x1, local copies, waits for them, and re-layouts, shards(): jnp.full((peers, capacity), -1, jnp.int32).at[owner, slot].set(doc_index)  21.2 us
    all_to_all x1, starting transfers between devices, shards(): lax.all_to_all(send_ids, 'docs', split_axis=0, concat_axis=0, tiled=True)  16.1 us
    all_to_all x1, starting transfers between devices, shards(): lax.all_to_all(send_rows, 'docs', split_axis=0, concat_axis=0, tiled=True)  13.4 us
  transfers between devices with their start and end apart: 3, of which 1 were waited for; matrix products, arithmetic and copies ran while one was open for 13% of the time, Pallas kernels for 0%

commit v1 on v0

--- a/solution.py
+++ b/solution.py
@@ -39,7 +39,9 @@
     doc_print = jnp.dot(member_table, got_rows, preferred_element_type=jnp.float32)
     high_part = doc_print.astype(jnp.bfloat16)
     low_part = (doc_print - high_part.astype(jnp.float32)).astype(jnp.bfloat16)
-    full_rows = lax.all_gather(query_pre, "docs", axis=1, tiled=True)
+    full_rows = jnp.concatenate(
+        lax.all_to_all(jnp.stack([query_pre] * lax.axis_size("docs")), "docs", 0, 0), axis=1
+    )
     scores = against_docs(
         lax.all_gather(full_rows, "blk", axis=0, tiled=True), high_part, low_part, weight
     )

time: 395 us -> 263 us (0.67)
  the two profiles are of different devices: /device:TPU:2 before, /device:TPU:1 now
where the time goes in v1:
time: 263 us; the launch traced here: 261 us
  waiting for transfers between devices  132 us (50%)
  local copies, waits for them, and re-layouts  72.7 us (28%)
  starting transfers between devices  35 us (13%)
  between operations  13.6 us (5%)
  matrix products  4.72 us (2%)
  other arithmetic  3.56 us (1%)
    all_to_all x1, waiting for transfers between devices, shards(): lax.all_to_all(send_rows, 'docs', split_axis=0, concat_axis=0, tiled=True)  121 us
    scatter x1, local copies, waits for them, and re-layouts, shards(): jnp.zeros((peers, capacity, width), jnp.bfloat16).at[owner, slot].set(rows)  44.5 us
    scatter x1, local copies, waits for them, and re-layouts, shards(): jnp.full((peers, capacity), -1, jnp.int32).at[owner, slot].set(doc_index)  21.2 us
    all_to_all x1, starting transfers between devices, shards(): lax.all_to_all(send_ids, 'docs', split_axis=0, concat_axis=0, tiled=True)  17 us
    all_to_all x1, starting transfers between devices, shards(): lax.all_to_all(send_rows, 'docs', split_axis=0, concat_axis=0, tiled=True)  13.2 us
    all_to_all x1, waiting for transfers between devices, shards(): lax.all_to_all(send_ids, 'docs', split_axis=0, concat_axis=0, tiled=True)  10.9 us
  transfers between devices with their start and end apart: 4, of which 2 were waited for; matrix products, arithmetic and copies ran while one was open for 20% of the time, Pallas kernels for 0%

profile of v1, /device:TPU:1, one launch (start us, length us, event | category | flops | bytes accessed | tf_op | source)
XLA Modules:
  0.0 261.3 jit_solution(16710313332681598361)
XLA Ops:
  6.5 0.7 fusion.11
  7.3 0.6 reduce-window.6
  7.9 0.2 slice_reduce_fusion
  8.1 0.8 fusion.10
  8.9 0.7 or_select_fusion
  9.6 21.2 %scatter_fusion = s32[64,8]{0,1:T(8,128)S(1)} fusion(s32[64,8]{0,1:T(8,128)S(1)} %broadcast_in_dim.6, s32[256]{0:T(256)S(1)} %bitcast.40, s32[256]{0:T(256)} %bitcast.47), kind=kCustom, calls=%fused_computation | custom fusion | bytes 5120 | tf_op jit(solution)/shard_map/scatter | solution.py:26
  30.8 0.0 copy-start.2
  30.8 0.7 copy.13
  31.5 17.0 %all-to-all-start.1 = ((s32[64,1,8]{2,1,0:T(1,128)}), s32[64,1,8]{2,1,0:T(1,128)S(1)}, u32[]{:S(2)}, u32[]{:S(2)}) async-start(s32[64,1,8]{2,1,0:T(1,128)} %copy.13), calls=%async_computation.1 | async-start | bytes 65536 | tf_op jit(solution)/shard_map/all_to_all | solution.py:34
  48.6 0.2 convolution_convert_fusion
  48.8 0.1 stack.2
  48.9 1.1 reshape.99
  49.9 10.9 %all-to-all-done.1 = s32[64,1,8]{2,1,0:T(1,128)S(1)} async-done(((s32[64,1,8]{2,1,0:T(1,128)}), s32[64,1,8]{2,1,0:T(1,128)S(1)}, u32[]{:S(2)}, u32[]{:S(2)}) %all-to-all-start.1) | async-done | bytes 2080 | tf_op jit(solution)/shard_map/all_to_all | solution.py:34
  60.8 4.7 %all-to-all-start = ((bf16[64,2,512]{2,1,0:T(2,128)(2,1)}), bf16[64,2,512]{2,1,0:T(2,128)(2,1)S(1)}, u32[]{:S(2)}, u32[]{:S(2)}) async-start(bf16[64,2,512]{2,1,0:T(2,128)(2,1)} %reshape.99), calls=%async_computation | async-start | bytes 262144 | tf_op jit(solution)/shard_map/all_to_all | solution.py:43
  65.5 1.6 broadcast_in_dim.7
  67.1 44.5 %scatter_fusion.1 = bf16[64,8,2048]{2,1,0:T(8,128)(2,1)} fusion(bf16[64,8,2048]{2,1,0:T(8,128)(2,1)} %broadcast_in_dim.7, s32[256]{0:T(256)S(1)} %bitcast.41, bf16[256,2048]{1,0:T(8,128)(2,1)S(1)} %bitcast.43), kind=kCustom, calls=%fused_computation.1 | custom fusion | bytes 3147776 | tf_op jit(solution)/shard_map/scatter | solution.py:31
  111.6 13.2 %all-to-all-start.2 = ((bf16[64,8,2048]{2,1,0:T(8,128)(2,1)}), bf16[64,8,2048]{2,1,0:T(8,128)(2,1)}, u32[]{:S(2)}, u32[]{:S(2)}) async-start(bf16[64,8,2048]{2,1,0:T(8,128)(2,1)} %scatter_fusion.1), calls=%async_computation.2 | async-start | bytes 4194304 | tf_op jit(solution)/shard_map/all_to_all | solution.py:33
  124.9 0.0 all-gather.2.cloned.1.call-start
  124.9 0.3 reshape.100
  125.2 0.2 copy.11
  125.4 1.2 reshape.74
  126.6 0.0 all-gather.2.cloned.1.call-update
  126.6 0.5 broadcast.103
  127.2 0.7 reduce.5
  127.9 0.1 eq.49
  128.0 120.9 %all-to-all-done.2 = bf16[64,8,2048]{2,1,0:T(8,128)(2,1)} async-done(((bf16[64,8,2048]{2,1,0:T(8,128)(2,1)}), bf16[64,8,2048]{2,1,0:T(8,128)(2,1)}, u32[]{:S(2)}, u32[]{:S(2)}) %all-to-all-start.2) | async-done | bytes 2097184 | tf_op jit(solution)/shard_map/all_to_all | solution.py:33
  248.8 2.3 fusion
  251.1 0.0 copy-start.4
  251.1 0.0 all-gather.2.cloned.1.call-done
  251.2 1.8 fusion.5
  253.0 0.5 fusion.3
  253.5 1.0 copy.14
  (12 shorter events, 0.1 us)
Async XLA Ops:
  6.5 42.1 %copy-start = (bf16[32,2048]{1,0:T(8,128)(2,1)S(1)}, bf16[32,2048]{1,0:T(8,128)(2,1)}, u32[]{:S(2)}) copy-start(bf16[32,2048]{1,0:T(8,128)(2,1)} %param.10) | copy-start | bytes 393220
  6.5 42.1 %copy-start.3 = (bf16[2048,32]{0,1:T(8,128)(2,1)S(1)}, bf16[2048,32]{0,1:T(8,128)(2,1)}, u32[]{:S(2)}) copy-start(bf16[2048,32]{0,1:T(8,128)(2,1)} %param.11) | copy-start | bytes 393220
  30.8 36.3 %copy-start.2 = (bf16[1,256,2048]{2,1,0:T(8,128)(2,1)S(1)}, bf16[1,256,2048]{2,1,0:T(8,128)(2,1)}, u32[]{:S(2)}) copy-start(bf16[1,256,2048]{2,1,0:T(8,128)(2,1)} %param.6) | copy-start | bytes 3145732
  31.5 29.3 %all-to-all-start.1 = ((s32[64,1,8]{2,1,0:T(1,128)}), s32[64,1,8]{2,1,0:T(1,128)S(1)}, u32[]{:S(2)}, u32[]{:S(2)}) async-start(s32[64,1,8]{2,1,0:T(1,128)} %copy.13), calls=%async_computation.1 | async-start | bytes 65536 | tf_op jit(solution)/shard_map/all_to_all | solution.py:34
  60.8 50.8 %all-to-all-start = ((bf16[64,2,512]{2,1,0:T(2,128)(2,1)}), bf16[64,2,512]{2,1,0:T(2,128)(2,1)S(1)}, u32[]{:S(2)}, u32[]{:S(2)}) async-start(bf16[64,2,512]{2,1,0:T(2,128)(2,1)} %reshape.99), calls=%async_computation | async-start | bytes 262144 | tf_op jit(solution)/shard_map/all_to_all | solution.py:43
  111.6 137.2 %all-to-all-start.2 = ((bf16[64,8,2048]{2,1,0:T(8,128)(2,1)}), bf16[64,8,2048]{2,1,0:T(8,128)(2,1)}, u32[]{:S(2)}, u32[]{:S(2)}) async-start(bf16[64,8,2048]{2,1,0:T(8,128)(2,1)} %scatter_fusion.1), calls=%async_computation.2 | async-start | bytes 4194304 | tf_op jit(solution)/shard_map/all_to_all | solution.py:33
  124.9 126.3 %all-gather.2.cloned.1.call-start = ((), (), s32[]{:S(2)}) async-start(), calls=%async_computation.3 | async-start | bytes 1179648 | tf_op jit(solution)/shard_map/all_gather | solution.py:46
  251.1 1.8 copy-start.4
  251.2 1.8 copy-start.1
Sparse Core Ops, SparseCore 0:
  128.9 85.7 all-gather.1
